TPU v7x, 32 devices: a whole 2x2x4 slice. The times are simulated.
32 devices in a mesh: row: 4 (over x, core), col: 8 (over z, y).
Axes of the slice: x: 2, y: 2, z: 4, core: 2. Of those that a mesh axis runs over, the one named last changes fastest.
Arguments:
- weight: bfloat16 [8192, 16384], P('row', 'col'), may hold values from -6 to 6
- gradient: bfloat16 [8192, 16384], P('row', 'col'), may hold values from -6 to 6
- old_basis: bfloat16 [8192, 1024], P('row'), may hold values from -0.0625 to 0.0625
- new_basis: bfloat16 [8192, 1024], P('row'), may hold values from -0.0625 to 0.0625
- first_moment: float32 [1024, 16384], P(None, ('col', 'row')), may hold values from -6 to 6
- second_moment: float32 [1024, 16384], P(None, ('col', 'row')), may hold values from 0.05 to 2
Outputs:
- new_weight: bfloat16 [8192, 16384], P('row', 'col')
- update: bfloat16 [8192, 16384], P('row', 'col')
- first_new: float32 [1024, 16384], P(None, ('col', 'row'))
- second_new: float32 [1024, 16384], P(None, ('col', 'row'))
All inputs are finite; a program needn't handle non-finite values.
Results may differ from a plain program's by a relative error of at most 0.0047.
Values may be sent and summed in bfloat16 or wider, within the bound.
A program may use at most 128 MiB of HBM per device.

v0:
```python
import jax
import jax.numpy as jnp
from jax import lax
from jax.sharding import PartitionSpec as P

beta_first = 0.9
beta_second = 0.95
epsilon = 1e-08
step_rate = 0.0025


def low(values):
    return values.astype(jnp.bfloat16)


def wide(values):
    return values.astype(jnp.float32)


def product(left, right):
    return jnp.einsum("mr,mn->rn", left, right, preferred_element_type=jnp.float32)


def transposed_transition(columns, old_basis, new_basis):
    part = old_basis.shape[1] // columns
    mine = lax.dynamic_slice_in_dim(old_basis, lax.axis_index("col") * part, part, axis=1)
    summed = lax.psum(product(mine, new_basis), "row")
    return lax.all_gather(low(summed), "col", axis=0, tiled=True)


def swaps(rows):
    core = [(r, r ^ 1) for r in range(rows)]
    chip = [(r, r ^ 2) for r in range(rows)]
    return (core, chip)


def shards(rows, columns, weight, gradient, old_basis, new_basis, first_moment, second_moment):
    flipped = transposed_transition(columns, old_basis, new_basis)
    squares = low(jnp.square(wide(flipped)))
    moved_first = product(flipped, low(first_moment))
    moved_second = product(squares, low(second_moment))
    width = first_moment.shape[1]
    row = lax.axis_index("row")
    here, core_mate, chip_mate, diagonal = (row ^ k for k in range(4)) if rows == 4 else (row,) * 4
    if rows == 4:
        core, chip = swaps(rows)

        def partial(block):
            piece = lax.dynamic_slice_in_dim(gradient, block * width, width, axis=1)
            return product(new_basis, piece)

        to_core_far = lax.ppermute(low(partial(diagonal)), "row", core)
        far = low(partial(chip_mate) + wide(to_core_far))
        from_chip = lax.ppermute(far, "row", chip)
        from_core = lax.ppermute(low(partial(core_mate)), "row", core)
        projected = partial(here) + wide(from_core) + wide(from_chip)
    else:
        sums = low(product(new_basis, gradient))
        projected = wide(lax.psum_scatter(sums, "row", scatter_dimension=1, tiled=True))
    first_new = beta_first * moved_first + (1.0 - beta_first) * projected
    second_new = beta_second * moved_second + (1.0 - beta_second) * projected * projected
    direction = low(first_new / (jnp.sqrt(second_new) + epsilon))
    if rows == 4:
        across = lax.ppermute(direction, "row", chip)
        beside = lax.ppermute(direction, "row", core)
        beyond = lax.ppermute(across, "row", core)
        directions = jnp.zeros((direction.shape[0], width * rows), direction.dtype)
        for block, values in (
            (here, direction),
            (core_mate, beside),
            (chip_mate, across),
            (diagonal, beyond),
        ):
            directions = lax.dynamic_update_slice_in_dim(directions, values, block * width, axis=1)
    else:
        directions = lax.all_gather(direction, "row", axis=1, tiled=True)
    back = jnp.dot(new_basis, directions, preferred_element_type=jnp.float32)
    new_weight = low(wide(weight) - step_rate * back)
    return (new_weight, low(back), first_new, second_new)


def solution(mesh):
    placed = (
        P("row", "col"),
        P("row", "col"),
        P("row", None),
        P("row", None),
        P(None, ("col", "row")),
        P(None, ("col", "row")),
    )
    return jax.shard_map(
        lambda *blocks: shards(mesh.shape["row"], mesh.shape["col"], *blocks),
        mesh=mesh,
        in_specs=placed,
        out_specs=(
            P("row", "col"),
            P("row", "col"),
            P(None, ("col", "row")),
            P(None, ("col", "row")),
        ),
        check_vma=False,
    )
```

profile of v0, /device:TPU:1, one launch (start us, length us, event | category | flops | bytes accessed | tf_op | source)
XLA Modules:
  0.0 180.5 jit_solution(16227457285369847139)
XLA Ops:
  7.2 0.0 all-gather.2.cloned.1.call-start
  7.2 3.1 %fusion.29 = f32[128,1024]{1,0:T(8,128)S(1)} fusion(bf16[2048,1024]{1,0:T(8,128)(2,1)} %param.9, bf16[2048,1024]{1,0:T(8,128)(2,1)} %param.8, s32[]{:T(128)S(6)} %select_n.19), kind=kOutput, calls=%fused_computation.27 | convolution fusion | flops 536870912 | bytes 5242884 | tf_op jit(solution)/shard_map/mr,mn->rn/dot_general | solution.py:21
  10.3 17.3 %all-reduce.1 = bf16[128,1024]{1,0:T(8,128)(2,1)} all-reduce(f32[128,1024]{1,0:T(8,128)S(1)} %fusion.29), channel_id=1, replica_groups=mesh['row'=4,'col'=8] {'row'}, use_global_device_ids=true, to_apply=%region_0.0 | all-reduce | flops 131072 | bytes 786432 | tf_op jit(solution)/shard_map/psum | solution.py:27
  27.6 0.0 all-gather.2.cloned.1.call-update
  27.6 5.2 %fusion.21 = bf16[1024,512]{1,0:T(8,128)(2,1)S(1)} fusion(bf16[2048,1024]{1,0:T(8,128)(2,1)} %param.9, bf16[2048,2048]{1,0:T(8,128)(2,1)} %param.7, s32[]{:T(128)S(6)} %select_n.23), kind=kOutput, calls=%fused_computation.23 | convolution fusion | flops 2148007936 | bytes 7340036 | tf_op jit(solution)/shard_map/mr,mn->rn/dot_general | solution.py:21
  32.9 1.9 %collective-permute-start.1 = (bf16[1024,512]{1,0:T(8,128)(2,1)S(1)}, bf16[1024,512]{1,0:T(8,128)(2,1)S(1)}, u32[]{:S(2)}, u32[]{:S(2)}) collective-permute-start(bf16[1024,512]{1,0:T(8,128)(2,1)S(1)} %fusion.21), channel_id=1, source_target_pairs={{0,8},{8,0},{16,24},{24,16},{1,9},{9,1},{17,25},{25,17},{2,10},{10... | collective-permute-start | bytes 3145736 | tf_op jit(solution)/shard_map/ppermute | solution.py:52
  34.7 6.3 %fusion.24 = bf16[1024,512]{1,0:T(8,128)(2,1)} fusion(bf16[2048,1024]{1,0:T(8,128)(2,1)} %param.9, bf16[2048,2048]{1,0:T(8,128)(2,1)} %param.7, s32[]{:T(128)S(6)} %select_n.21), kind=kOutput, calls=%fused_computation.24 | convolution fusion | flops 2148007936 | bytes 7340036 | tf_op jit(solution)/shard_map/mr,mn->rn/dot_general | solution.py:21
  41.0 0.0 collective-permute-start
  41.0 0.0 collective-permute-done.1
  41.0 6.2 %fusion.3 = bf16[1024,512]{1,0:T(8,128)(2,1)} fusion(bf16[1024,512]{1,0:T(8,128)(2,1)S(1)} %collective-permute-done.1, bf16[2048,1024]{1,0:T(8,128)(2,1)} %param.9, bf16[2048,2048]{1,0:T(8,128)(2,1)} %param.7, s32[]{:T(128)S(6)} %select_n.22), kind=kOutput, calls=%fused_computation.8 | convolution fusion | flops 2149056512 | bytes 8388612 | tf_op jit(solution)/shard_map/mr,mn->rn/dot_general | solution.py:21
  47.2 0.6 collective-permute-start.2
  47.8 0.0 copy-start.1
  47.8 6.7 %fusion.11 = f32[512,1024]{0,1:T(8,128)} fusion(bf16[2048,1024]{1,0:T(8,128)(2,1)} %param.9, bf16[2048,2048]{1,0:T(8,128)(2,1)} %param.7, s32[]{:T(128)S(6)} %select_n.20), kind=kOutput, calls=%fused_computation.19 | convolution fusion | flops 2147483648 | bytes 8388612 | tf_op jit(solution)/shard_map/mr,mn->rn/dot_general | solution.py:21
  54.5 0.0 collective-permute-done
  54.5 17.3 %collective-permute-done.2 = bf16[1024,512]{1,0:T(8,128)(2,1)} collective-permute-done((bf16[1024,512]{1,0:T(8,128)(2,1)}, bf16[1024,512]{1,0:T(8,128)(2,1)}, u32[]{:S(2)}, u32[]{:S(2)}) %collective-permute-start.2) | collective-permute-done | bytes 1048608 | tf_op jit(solution)/shard_map/ppermute | solution.py:54
  71.8 4.9 %all-gather.2.cloned.1.call-done = bf16[1024,1024]{1,0:T(8,128)(2,1)} async-done(((bf16[128,1024]{1,0:T(8,128)(2,1)}), bf16[1024,1024]{1,0:T(8,128)(2,1)}) %all-gather.2.cloned.1.call-update) | async-done | bytes 2097168 | tf_op jit(solution)/shard_map/all_gather | solution.py:28
  76.7 0.0 copy-done.1
  76.7 0.0 copy-start.5
  76.7 4.2 %fusion.1 = f32[1024,512]{1,0:T(8,128)S(1)} fusion(bf16[1024,1024]{1,0:T(8,128)(2,1)} %all-gather.2.cloned.1.call-done, f32[1024,512]{1,0:T(8,128)S(1)} %copy-done.1, bf16[1024,512]{1,0:T(8,128)(2,1)} %collective-permute-done.2, bf16[1024,512]{1,0:T(8,128)(2,1)S(1)} %collective-permute-done, f32[512,1024]{0,1:T(8,128)} %fusion.11), kind=kOutput, calls=%fused_computation.5 | convolution fusion | flops 1081606144 | bytes 10485760 | tf_op jit(solution)/shard_map/mr,mn->rn/dot_general | solution.py:21
  80.9 0.0 copy-start.4
  80.9 0.0 copy-start.2
  80.9 0.0 copy-start.3
  81.0 2.7 %broadcast_in_dim.3 = bf16[1024,2048]{1,0:T(8,128)(2,1)} broadcast(bf16[]{:T(256)} %constant.17.clone.1), dimensions={} | broadcast | bytes 4194306 | tf_op jit(solution)/shard_map/broadcast_in_dim | solution.py:67
  83.6 0.0 copy-done.5
  83.6 0.5 copy-done.2
  84.1 1.3 copy-done.3
  85.4 5.5 %constant_dynamic-update-slice_fusion.3 = (bf16[1024,2048]{1,0:T(8,128)(2,1)}, bf16[1024,512]{1,0:T(8,128)(2,1)}, f32[1024,512]{1,0:T(8,128)}) fusion(bf16[1024,2048]{1,0:T(8,128)(2,1)} %broadcast_in_dim.3, s32[]{:T(128)S(6)} %select_n.20, f32[1024,512]{1,0:T(8,128)S(1)} %fusion.1, bf16[1024,512]{1,0:T(8,128)(2,1)} %collective-permute-done.2, ...), kind=kOutput, calls=%fused_computation.32 | convolution fusion | flops 1079508992 | bytes 14680068 | tf_op jit(solution)/shard_map/mr,mn->rn/dot_general | solution.py:21
  91.0 0.0 copy-done.4
  91.0 1.2 collective-permute-start.4
  92.2 2.9 %collective-permute-start.3 = (bf16[1024,512]{1,0:T(8,128)(2,1)}, bf16[1024,512]{1,0:T(8,128)(2,1)S(1)}, u32[]{:S(2)}, u32[]{:S(2)}) collective-permute-start(bf16[1024,512]{1,0:T(8,128)(2,1)} %get-tuple-element.9), channel_id=1, source_target_pairs={{0,8},{8,0},{16,24},{24,16},{1,9},{9,1},{17,25},{25,17},{2,10},{10... | collective-permute-start | bytes 3145736 | tf_op jit(solution)/shard_map/ppermute | solution.py:65
  95.0 18.3 %collective-permute-done.4 = bf16[1024,512]{1,0:T(8,128)(2,1)S(1)} collective-permute-done((bf16[1024,512]{1,0:T(8,128)(2,1)}, bf16[1024,512]{1,0:T(8,128)(2,1)S(1)}, u32[]{:S(2)}, u32[]{:S(2)}) %collective-permute-start.4) | collective-permute-done | bytes 1048608 | tf_op jit(solution)/shard_map/ppermute | solution.py:64
  113.3 3.4 %collective-permute-start.5 = (bf16[1024,512]{1,0:T(8,128)(2,1)S(1)}, bf16[1024,512]{1,0:T(8,128)(2,1)S(1)}, u32[]{:S(2)}, u32[]{:S(2)}) collective-permute-start(bf16[1024,512]{1,0:T(8,128)(2,1)S(1)} %collective-permute-done.4), channel_id=1, source_target_pairs={{0,8},{8,0},{16,24},{24,16},{1,9},{9,1},{17,25},{25,17},{2,10},{10... | collective-permute-start | bytes 3145736 | tf_op jit(solution)/shard_map/ppermute | solution.py:66
  116.8 12.2 %copy.10 = bf16[2048,2048]{0,1:T(8,128)(2,1)} copy(bf16[2048,2048]{1,0:T(8,128)(2,1)} %param.6) | data formatting | bytes 16777216 | tf_op args[0]
  129.0 0.0 copy-start
  129.0 0.0 collective-permute-done.3
  129.0 1.0 constant_dynamic-update-slice_fusion.2
  130.0 1.0 constant_dynamic-update-slice_fusion.1
  131.1 0.0 collective-permute-done.5
  131.1 1.0 constant_dynamic-update-slice_fusion
  132.1 0.0 copy-done
  132.1 17.1 %fusion = (bf16[2048,2048]{0,1:T(8,128)(2,1)}, bf16[2048,2048]{1,0:T(8,128)(2,1)}) fusion(bf16[2048,2048]{0,1:T(8,128)(2,1)} %copy.10, bf16[1024,2048]{1,0:T(8,128)(2,1)} %constant_dynamic-update-slice_fusion, bf16[2048,1024]{1,0:T(8,128)(2,1)S(1)} %copy-done), kind=kOutput, calls=%fused_computation.1 | convolution fusion | flops 8610906112 | bytes 33554432 | tf_op jit(solution)/shard_map/dot_general | solution.py:77
  149.2 12.2 %copy.15 = bf16[2048,2048]{1,0:T(8,128)(2,1)} copy(bf16[2048,2048]{0,1:T(8,128)(2,1)} %get-tuple-element.11) | data formatting | bytes 16777216
  161.5 12.2 %copy.16 = bf16[2048,2048]{1,0:T(8,128)(2,1)} copy(bf16[2048,2048]{0,1:T(8,128)(2,1)} %bitcast.31) | data formatting | bytes 16777216
Async XLA Ops:
  7.2 69.5 %all-gather.2.cloned.1.call-start = ((), (), s32[]{:S(2)}) async-start(), calls=%async_computation | async-start | bytes 2359296 | tf_op jit(solution)/shard_map/all_gather | solution.py:28
  32.9 8.1 %collective-permute-start.1 = (bf16[1024,512]{1,0:T(8,128)(2,1)S(1)}, bf16[1024,512]{1,0:T(8,128)(2,1)S(1)}, u32[]{:S(2)}, u32[]{:S(2)}) collective-permute-start(bf16[1024,512]{1,0:T(8,128)(2,1)S(1)} %fusion.21), channel_id=1, source_target_pairs={{0,8},{8,0},{16,24},{24,16},{1,9},{9,1},{17,25},{25,17},{2,10},{10... | collective-permute-start | bytes 3145736 | tf_op jit(solution)/shard_map/ppermute | solution.py:52
  41.0 13.5 %collective-permute-start = (bf16[1024,512]{1,0:T(8,128)(2,1)}, bf16[1024,512]{1,0:T(8,128)(2,1)S(1)}, u32[]{:S(2)}, u32[]{:S(2)}) collective-permute-start(bf16[1024,512]{1,0:T(8,128)(2,1)} %fusion.24), channel_id=1, source_target_pairs={{0,8},{8,0},{16,24},{24,16},{1,9},{9,1},{17,25},{25,17},{2,10},{10... | collective-permute-start | bytes 3145736 | tf_op jit(solution)/shard_map/ppermute | solution.py:55
  47.2 24.5 %collective-permute-start.2 = (bf16[1024,512]{1,0:T(8,128)(2,1)}, bf16[1024,512]{1,0:T(8,128)(2,1)}, u32[]{:S(2)}, u32[]{:S(2)}) collective-permute-start(bf16[1024,512]{1,0:T(8,128)(2,1)} %fusion.3), channel_id=1, source_target_pairs={{0,16},{8,24},{16,0},{24,8},{1,17},{9,25},{17,1},{25,9},{2,18},{10... | collective-permute-start | bytes 3145736 | tf_op jit(solution)/shard_map/ppermute | solution.py:54
  47.8 28.9 %copy-start.1 = (f32[1024,512]{1,0:T(8,128)S(1)}, f32[1024,512]{1,0:T(8,128)}, u32[]{:S(2)}) copy-start(f32[1024,512]{1,0:T(8,128)} %param.11) | copy-start | bytes 6291460
  76.7 6.9 %copy-start.5 = (f32[512,1024]{0,1:T(8,128)S(1)}, f32[512,1024]{0,1:T(8,128)}, u32[]{:S(2)}) copy-start(f32[512,1024]{0,1:T(8,128)} %fusion.11) | copy-start | bytes 6291460
  80.9 10.0 %copy-start.4 = (f32[1024,512]{1,0:T(8,128)}, f32[1024,512]{1,0:T(8,128)S(1)}, u32[]{:S(2)}) copy-start(f32[1024,512]{1,0:T(8,128)S(1)} %fusion.1) | copy-start | bytes 6291460
  80.9 3.2 %copy-start.2 = (f32[1024,512]{1,0:T(8,128)S(1)}, f32[1024,512]{1,0:T(8,128)}, u32[]{:S(2)}) copy-start(f32[1024,512]{1,0:T(8,128)} %param.10) | copy-start | bytes 6291460
  80.9 4.5 %copy-start.3 = (bf16[1024,1024]{1,0:T(8,128)(2,1)S(1)}, bf16[1024,1024]{1,0:T(8,128)(2,1)}, u32[]{:S(2)}) copy-start(bf16[1024,1024]{1,0:T(8,128)(2,1)} %all-gather.2.cloned.1.call-done) | copy-start | bytes 6291460
  91.0 22.3 %collective-permute-start.4 = (bf16[1024,512]{1,0:T(8,128)(2,1)}, bf16[1024,512]{1,0:T(8,128)(2,1)S(1)}, u32[]{:S(2)}, u32[]{:S(2)}) collective-permute-start(bf16[1024,512]{1,0:T(8,128)(2,1)} %get-tuple-element.9), channel_id=1, source_target_pairs={{0,16},{8,24},{16,0},{24,8},{1,17},{9,25},{17,1},{25,9},{2,18},{10... | collective-permute-start | bytes 3145736 | tf_op jit(solution)/shard_map/ppermute | solution.py:64
  92.2 36.8 %collective-permute-start.3 = (bf16[1024,512]{1,0:T(8,128)(2,1)}, bf16[1024,512]{1,0:T(8,128)(2,1)S(1)}, u32[]{:S(2)}, u32[]{:S(2)}) collective-permute-start(bf16[1024,512]{1,0:T(8,128)(2,1)} %get-tuple-element.9), channel_id=1, source_target_pairs={{0,8},{8,0},{16,24},{24,16},{1,9},{9,1},{17,25},{25,17},{2,10},{10... | collective-permute-start | bytes 3145736 | tf_op jit(solution)/shard_map/ppermute | solution.py:65
  113.3 17.8 %collective-permute-start.5 = (bf16[1024,512]{1,0:T(8,128)(2,1)S(1)}, bf16[1024,512]{1,0:T(8,128)(2,1)S(1)}, u32[]{:S(2)}, u32[]{:S(2)}) collective-permute-start(bf16[1024,512]{1,0:T(8,128)(2,1)S(1)} %collective-permute-done.4), channel_id=1, source_target_pairs={{0,8},{8,0},{16,24},{24,16},{1,9},{9,1},{17,25},{25,17},{2,10},{10... | collective-permute-start | bytes 3145736 | tf_op jit(solution)/shard_map/ppermute | solution.py:66
  129.0 3.1 %copy-start = (bf16[2048,1024]{1,0:T(8,128)(2,1)S(1)}, bf16[2048,1024]{1,0:T(8,128)(2,1)}, u32[]{:S(2)}) copy-start(bf16[2048,1024]{1,0:T(8,128)(2,1)} %param.9) | copy-start | bytes 12582916
Sparse Core Ops, SparseCore 0:
  27.7 48.8 all-gather.1
where the time goes:
time: 182 us; the launch traced here: 181 us
  matrix products  54.4 us (30%)
  local copies, waits for them, and re-layouts  44.3 us (24%)
  waiting for transfers between devices  40.5 us (22%)
  blocking collectives  17.3 us (10%)
  between operations  14.1 us (8%)
  starting transfers between devices  10 us (5%)
    unnamed x15, local copies, waits for them, and re-layouts  38.5 us
    dot_general x7, matrix products, product(): jnp.einsum('mr,mn->rn', left, right, preferred_element_type=jnp.float32)  37.2 us
    ppermute x1, waiting for transfers between devices, shards(): across = lax.ppermute(direction, 'row', chip)  18.3 us
    ppermute x1, waiting for transfers between devices, shards(): from_chip = lax.ppermute(far, 'row', chip)  17.3 us
    psum x1, blocking collectives, transposed_transition(): summed = lax.psum(product(mine, new_basis), 'row')  17.3 us
    dot_general x1, matrix products, shards(): back = jnp.dot(new_basis, directions, preferred_element_type=jnp.float32)  17.1 us
    all_gather x1, waiting for transfers between devices, transposed_transition(): return lax.all_gather(low(summed), 'col', axis=0, tiled=True)  4.92 us
  transfers between devices with their start and end apart: 7, of which 3 were waited for; matrix products, arithmetic and copies ran while one was open for 21% of the time, Pallas kernels for 0%

commit v1 on v0

--- a/solution.py
+++ b/solution.py
@@ -24,7 +24,8 @@
 def transposed_transition(columns, old_basis, new_basis):
     part = old_basis.shape[1] // columns
     mine = lax.dynamic_slice_in_dim(old_basis, lax.axis_index("col") * part, part, axis=1)
-    summed = lax.psum(product(mine, new_basis), "row")
+    xin = product(mine, new_basis)
+    summed = lax.all_gather(xin, "row").sum(axis=0)
     return lax.all_gather(low(summed), "col", axis=0, tiled=True)
 
 

time: 182 us -> 191 us (1.049)
  waiting for transfers between devices: 40.5 us -> 65.3 us
  blocking collectives: 17.3 us -> 0 us
  other arithmetic: 0 us -> 2.53 us
    all_gather x0 -> x1, waiting for transfers between devices: none -> 25.1 us  [transposed_transition(): summed = lax.all_gather(xin, 'row').sum(axis=0)]
    psum x1 -> x0, blocking collectives: 17.3 us -> none  [transposed_transition(): summed = lax.psum(product(mine, new_basis), 'row')]
    reduce_sum x0 -> x1, other arithmetic: none -> 2.53 us  [transposed_transition(): summed = lax.all_gather(xin, 'row').sum(axis=0)]
  transfers between devices with their start and end apart: 7 -> 8, of which waited for: 3 -> 4; matrix products, arithmetic and copies ran while one was open for 21% -> 20% of each run, Pallas kernels for 0% -> 0%
where the time goes in v1:
time: 191 us; the launch traced here: 190 us
  waiting for transfers between devices  65.3 us (34%)
  matrix products  55.3 us (29%)
  local copies, waits for them, and re-layouts  44.3 us (23%)
  between operations  14.1 us (7%)
  starting transfers between devices  8.18 us (4%)
  other arithmetic  2.53 us (1%)
    unnamed x15, local copies, waits for them, and re-layouts  38.5 us
    dot_general x7, matrix products, product(): jnp.einsum('mr,mn->rn', left, right, preferred_element_type=jnp.float32)  38.1 us
    all_gather x1, waiting for transfers between devices, transposed_transition(): summed = lax.all_gather(xin, 'row').sum(axis=0)  25.1 us
    ppermute x1, waiting for transfers between devices, shards(): across = lax.ppermute(direction, 'row', chip)  18.3 us
    ppermute x1, waiting for transfers between devices, shards(): from_chip = lax.ppermute(far, 'row', chip)  18.1 us
    dot_general x1, matrix products, shards(): back = jnp.dot(new_basis, directions, preferred_element_type=jnp.float32)  17.1 us
  transfers between devices with their start and end apart: 8, of which 4 were waited for; matrix products, arithmetic and copies ran while one was open for 20% of the time, Pallas kernels for 0%

profile of v1, /device:TPU:1, one launch (start us, length us, event | category | flops | bytes accessed | tf_op | source)
XLA Modules:
  0.0 189.7 jit_solution(9705743622113435033)
XLA Ops:
  7.2 0.0 all-gather.6.cloned.1.call-start
  7.2 3.9 %fusion.29 = f32[128,1024]{1,0:T(8,128)} fusion(bf16[2048,1024]{1,0:T(8,128)(2,1)} %param.9, bf16[2048,1024]{1,0:T(8,128)(2,1)} %param.8, s32[]{:T(128)S(6)} %select_n.19), kind=kOutput, calls=%fused_computation.27 | convolution fusion | flops 536870912 | bytes 5242884 | tf_op jit(solution)/shard_map/mr,mn->rn/dot_general | solution.py:21
  11.1 0.0 all-gather.6.cloned.1.call-update
  11.2 0.0 all-gather.4.cloned.1.call-start
  11.2 25.1 %all-gather.6.cloned.1.call-done = f32[512,1024]{1,0:T(8,128)} async-done(((f32[128,1024]{1,0:T(8,128)}), f32[512,1024]{1,0:T(8,128)}) %all-gather.6.cloned.1.call-update) | async-done | bytes 2097168 | tf_op jit(solution)/shard_map/all_gather | solution.py:28
  36.3 2.5 %reduce_sum.9 = bf16[128,1024]{1,0:T(8,128)(2,1)} reduce(f32[4,128,1024]{2,1,0:T(8,128)} %bitcast.33, f32[]{:T(128)} %constant.7.clone.1), dimensions={0}, to_apply=%region_0.0 | reduce | flops 393216 | bytes 2359300 | tf_op jit(solution)/shard_map/reduce_sum | solution.py:28
  38.9 0.0 all-gather.4.cloned.1.call-update
  38.9 5.2 %fusion.21 = bf16[1024,512]{1,0:T(8,128)(2,1)S(1)} fusion(bf16[2048,1024]{1,0:T(8,128)(2,1)} %param.9, bf16[2048,2048]{1,0:T(8,128)(2,1)} %param.7, s32[]{:T(128)S(6)} %select_n.23), kind=kOutput, calls=%fused_computation.23 | convolution fusion | flops 2148007936 | bytes 7340036 | tf_op jit(solution)/shard_map/mr,mn->rn/dot_general | solution.py:21
  44.1 0.3 collective-permute-start.1
  44.5 6.3 %fusion.24 = bf16[1024,512]{1,0:T(8,128)(2,1)} fusion(bf16[2048,1024]{1,0:T(8,128)(2,1)} %param.9, bf16[2048,2048]{1,0:T(8,128)(2,1)} %param.7, s32[]{:T(128)S(6)} %select_n.21), kind=kOutput, calls=%fused_computation.24 | convolution fusion | flops 2148007936 | bytes 7340036 | tf_op jit(solution)/shard_map/mr,mn->rn/dot_general | solution.py:21
  50.8 0.2 collective-permute-start
  51.0 0.0 collective-permute-done.1
  51.0 6.2 %fusion.3 = bf16[1024,512]{1,0:T(8,128)(2,1)} fusion(bf16[1024,512]{1,0:T(8,128)(2,1)S(1)} %collective-permute-done.1, bf16[2048,1024]{1,0:T(8,128)(2,1)} %param.9, bf16[2048,2048]{1,0:T(8,128)(2,1)} %param.7, s32[]{:T(128)S(6)} %select_n.22), kind=kOutput, calls=%fused_computation.8 | convolution fusion | flops 2149056512 | bytes 8388612 | tf_op jit(solution)/shard_map/mr,mn->rn/dot_general | solution.py:21
  57.3 0.0 collective-permute-start.2
  57.3 0.0 copy-start.1
  57.3 6.7 %fusion.11 = f32[512,1024]{0,1:T(8,128)} fusion(bf16[2048,1024]{1,0:T(8,128)(2,1)} %param.9, bf16[2048,2048]{1,0:T(8,128)(2,1)} %param.7, s32[]{:T(128)S(6)} %select_n.20), kind=kOutput, calls=%fused_computation.19 | convolution fusion | flops 2147483648 | bytes 8388612 | tf_op jit(solution)/shard_map/mr,mn->rn/dot_general | solution.py:21
  64.0 0.0 collective-permute-done
  64.0 18.1 %collective-permute-done.2 = bf16[1024,512]{1,0:T(8,128)(2,1)} collective-permute-done((bf16[1024,512]{1,0:T(8,128)(2,1)}, bf16[1024,512]{1,0:T(8,128)(2,1)}, u32[]{:S(2)}, u32[]{:S(2)}) %collective-permute-start.2) | collective-permute-done | bytes 1048608 | tf_op jit(solution)/shard_map/ppermute | solution.py:55
  82.0 3.8 %all-gather.4.cloned.1.call-done = bf16[1024,1024]{1,0:T(8,128)(2,1)} async-done(((bf16[128,1024]{1,0:T(8,128)(2,1)}), bf16[1024,1024]{1,0:T(8,128)(2,1)}) %all-gather.4.cloned.1.call-update) | async-done | bytes 2097168 | tf_op jit(solution)/shard_map/all_gather | solution.py:29
  85.8 0.0 copy-done.1
  85.8 0.0 copy-start.5
  85.8 4.2 %fusion.1 = f32[1024,512]{1,0:T(8,128)S(1)} fusion(bf16[1024,1024]{1,0:T(8,128)(2,1)} %all-gather.4.cloned.1.call-done, f32[1024,512]{1,0:T(8,128)S(1)} %copy-done.1, bf16[1024,512]{1,0:T(8,128)(2,1)} %collective-permute-done.2, bf16[1024,512]{1,0:T(8,128)(2,1)S(1)} %collective-permute-done, f32[512,1024]{0,1:T(8,128)} %fusion.11), kind=kOutput, calls=%fused_computation.5 | convolution fusion | flops 1081606144 | bytes 10485760 | tf_op jit(solution)/shard_map/mr,mn->rn/dot_general | solution.py:21
  90.1 0.0 copy-start.4
  90.1 0.0 copy-start.2
  90.1 0.0 copy-start.3
  90.1 2.7 %broadcast_in_dim.3 = bf16[1024,2048]{1,0:T(8,128)(2,1)} broadcast(bf16[]{:T(256)} %constant.18.clone.1), dimensions={} | broadcast | bytes 4194306 | tf_op jit(solution)/shard_map/broadcast_in_dim | solution.py:68
  92.8 0.0 copy-done.5
  92.8 0.5 copy-done.2
  93.2 1.3 copy-done.3
  94.6 5.6 %constant_dynamic-update-slice_fusion.3 = (bf16[1024,2048]{1,0:T(8,128)(2,1)}, bf16[1024,512]{1,0:T(8,128)(2,1)}, f32[1024,512]{1,0:T(8,128)}) fusion(bf16[1024,2048]{1,0:T(8,128)(2,1)} %broadcast_in_dim.3, s32[]{:T(128)S(6)} %select_n.20, f32[1024,512]{1,0:T(8,128)S(1)} %fusion.1, bf16[1024,512]{1,0:T(8,128)(2,1)} %collective-permute-done.2, ...), kind=kOutput, calls=%fused_computation.32 | convolution fusion | flops 1079508992 | bytes 14680068 | tf_op jit(solution)/shard_map/mr,mn->rn/dot_general | solution.py:21
  100.1 0.0 copy-done.4
  100.1 1.2 collective-permute-start.4
  101.3 2.9 %collective-permute-start.3 = (bf16[1024,512]{1,0:T(8,128)(2,1)}, bf16[1024,512]{1,0:T(8,128)(2,1)S(1)}, u32[]{:S(2)}, u32[]{:S(2)}) collective-permute-start(bf16[1024,512]{1,0:T(8,128)(2,1)} %get-tuple-element.9), channel_id=1, source_target_pairs={{0,8},{8,0},{16,24},{24,16},{1,9},{9,1},{17,25},{25,17},{2,10},{10... | collective-permute-start | bytes 3145736 | tf_op jit(solution)/shard_map/ppermute | solution.py:66
  104.2 18.3 %collective-permute-done.4 = bf16[1024,512]{1,0:T(8,128)(2,1)S(1)} collective-permute-done((bf16[1024,512]{1,0:T(8,128)(2,1)}, bf16[1024,512]{1,0:T(8,128)(2,1)S(1)}, u32[]{:S(2)}, u32[]{:S(2)}) %collective-permute-start.4) | collective-permute-done | bytes 1048608 | tf_op jit(solution)/shard_map/ppermute | solution.py:65
  122.5 3.5 %collective-permute-start.5 = (bf16[1024,512]{1,0:T(8,128)(2,1)S(1)}, bf16[1024,512]{1,0:T(8,128)(2,1)S(1)}, u32[]{:S(2)}, u32[]{:S(2)}) collective-permute-start(bf16[1024,512]{1,0:T(8,128)(2,1)S(1)} %collective-permute-done.4), channel_id=1, source_target_pairs={{0,8},{8,0},{16,24},{24,16},{1,9},{9,1},{17,25},{25,17},{2,10},{10... | collective-permute-start | bytes 3145736 | tf_op jit(solution)/shard_map/ppermute | solution.py:67
  125.9 12.2 %copy.10 = bf16[2048,2048]{0,1:T(8,128)(2,1)} copy(bf16[2048,2048]{1,0:T(8,128)(2,1)} %param.6) | data formatting | bytes 16777216 | tf_op args[0]
  138.2 0.0 copy-start
  138.2 0.0 collective-permute-done.3
  138.2 1.0 constant_dynamic-update-slice_fusion.2
  139.2 1.0 constant_dynamic-update-slice_fusion.1
  140.2 0.0 collective-permute-done.5
  140.2 1.0 constant_dynamic-update-slice_fusion
  141.3 0.0 copy-done
  141.3 17.1 %fusion = (bf16[2048,2048]{0,1:T(8,128)(2,1)}, bf16[2048,2048]{1,0:T(8,128)(2,1)}) fusion(bf16[2048,2048]{0,1:T(8,128)(2,1)} %copy.10, bf16[1024,2048]{1,0:T(8,128)(2,1)} %constant_dynamic-update-slice_fusion, bf16[2048,1024]{1,0:T(8,128)(2,1)S(1)} %copy-done), kind=kOutput, calls=%fused_computation.1 | convolution fusion | flops 8610906112 | bytes 33554432 | tf_op jit(solution)/shard_map/dot_general | solution.py:78
  158.4 12.2 %copy.15 = bf16[2048,2048]{1,0:T(8,128)(2,1)} copy(bf16[2048,2048]{0,1:T(8,128)(2,1)} %get-tuple-element.11) | data formatting | bytes 16777216
  170.6 12.2 %copy.16 = bf16[2048,2048]{1,0:T(8,128)(2,1)} copy(bf16[2048,2048]{0,1:T(8,128)(2,1)} %bitcast.32) | data formatting | bytes 16777216
Async XLA Ops:
  7.2 29.2 %all-gather.6.cloned.1.call-start = ((), (), s32[]{:S(2)}) async-start(), calls=%async_computation.1 | async-start | bytes 2621440 | tf_op jit(solution)/shard_map/all_gather | solution.py:28
  11.2 74.7 %all-gather.4.cloned.1.call-start = ((), (), s32[]{:S(2)}) async-start(), calls=%async_computation | async-start | bytes 2359296 | tf_op jit(solution)/shard_map/all_gather | solution.py:29
  44.1 6.9 %collective-permute-start.1 = (bf16[1024,512]{1,0:T(8,128)(2,1)S(1)}, bf16[1024,512]{1,0:T(8,128)(2,1)S(1)}, u32[]{:S(2)}, u32[]{:S(2)}) collective-permute-start(bf16[1024,512]{1,0:T(8,128)(2,1)S(1)} %fusion.21), channel_id=1, source_target_pairs={{0,8},{8,0},{16,24},{24,16},{1,9},{9,1},{17,25},{25,17},{2,10},{10... | collective-permute-start | bytes 3145736 | tf_op jit(solution)/shard_map/ppermute | solution.py:53
  50.8 13.2 %collective-permute-start = (bf16[1024,512]{1,0:T(8,128)(2,1)}, bf16[1024,512]{1,0:T(8,128)(2,1)S(1)}, u32[]{:S(2)}, u32[]{:S(2)}) collective-permute-start(bf16[1024,512]{1,0:T(8,128)(2,1)} %fusion.24), channel_id=1, source_target_pairs={{0,8},{8,0},{16,24},{24,16},{1,9},{9,1},{17,25},{25,17},{2,10},{10... | collective-permute-start | bytes 3145736 | tf_op jit(solution)/shard_map/ppermute | solution.py:56
  57.3 24.8 %collective-permute-start.2 = (bf16[1024,512]{1,0:T(8,128)(2,1)}, bf16[1024,512]{1,0:T(8,128)(2,1)}, u32[]{:S(2)}, u32[]{:S(2)}) collective-permute-start(bf16[1024,512]{1,0:T(8,128)(2,1)} %fusion.3), channel_id=1, source_target_pairs={{0,16},{8,24},{16,0},{24,8},{1,17},{9,25},{17,1},{25,9},{2,18},{10... | collective-permute-start | bytes 3145736 | tf_op jit(solution)/shard_map/ppermute | solution.py:55
  57.3 28.6 %copy-start.1 = (f32[1024,512]{1,0:T(8,128)S(1)}, f32[1024,512]{1,0:T(8,128)}, u32[]{:S(2)}) copy-start(f32[1024,512]{1,0:T(8,128)} %param.11) | copy-start | bytes 6291460
  85.8 6.9 %copy-start.5 = (f32[512,1024]{0,1:T(8,128)S(1)}, f32[512,1024]{0,1:T(8,128)}, u32[]{:S(2)}) copy-start(f32[512,1024]{0,1:T(8,128)} %fusion.11) | copy-start | bytes 6291460
  90.1 10.1 %copy-start.4 = (f32[1024,512]{1,0:T(8,128)}, f32[1024,512]{1,0:T(8,128)S(1)}, u32[]{:S(2)}) copy-start(f32[1024,512]{1,0:T(8,128)S(1)} %fusion.1) | copy-start | bytes 6291460
  90.1 3.2 %copy-start.2 = (f32[1024,512]{1,0:T(8,128)S(1)}, f32[1024,512]{1,0:T(8,128)}, u32[]{:S(2)}) copy-start(f32[1024,512]{1,0:T(8,128)} %param.10) | copy-start | bytes 6291460
  90.1 4.5 %copy-start.3 = (bf16[1024,1024]{1,0:T(8,128)(2,1)S(1)}, bf16[1024,1024]{1,0:T(8,128)(2,1)}, u32[]{:S(2)}) copy-start(bf16[1024,1024]{1,0:T(8,128)(2,1)} %all-gather.4.cloned.1.call-done) | copy-start | bytes 6291460
  100.1 22.3 %collective-permute-start.4 = (bf16[1024,512]{1,0:T(8,128)(2,1)}, bf16[1024,512]{1,0:T(8,128)(2,1)S(1)}, u32[]{:S(2)}, u32[]{:S(2)}) collective-permute-start(bf16[1024,512]{1,0:T(8,128)(2,1)} %get-tuple-element.9), channel_id=1, source_target_pairs={{0,16},{8,24},{16,0},{24,8},{1,17},{9,25},{17,1},{25,9},{2,18},{10... | collective-permute-start | bytes 3145736 | tf_op jit(solution)/shard_map/ppermute | solution.py:65
  101.3 36.8 %collective-permute-start.3 = (bf16[1024,512]{1,0:T(8,128)(2,1)}, bf16[1024,512]{1,0:T(8,128)(2,1)S(1)}, u32[]{:S(2)}, u32[]{:S(2)}) collective-permute-start(bf16[1024,512]{1,0:T(8,128)(2,1)} %get-tuple-element.9), channel_id=1, source_target_pairs={{0,8},{8,0},{16,24},{24,16},{1,9},{9,1},{17,25},{25,17},{2,10},{10... | collective-permute-start | bytes 3145736 | tf_op jit(solution)/shard_map/ppermute | solution.py:66
  122.5 17.8 %collective-permute-start.5 = (bf16[1024,512]{1,0:T(8,128)(2,1)S(1)}, bf16[1024,512]{1,0:T(8,128)(2,1)S(1)}, u32[]{:S(2)}, u32[]{:S(2)}) collective-permute-start(bf16[1024,512]{1,0:T(8,128)(2,1)S(1)} %collective-permute-done.4), channel_id=1, source_target_pairs={{0,8},{8,0},{16,24},{24,16},{1,9},{9,1},{17,25},{25,17},{2,10},{10... | collective-permute-start | bytes 3145736 | tf_op jit(solution)/shard_map/ppermute | solution.py:67
  138.2 3.1 %copy-start = (bf16[2048,1024]{1,0:T(8,128)(2,1)S(1)}, bf16[2048,1024]{1,0:T(8,128)(2,1)}, u32[]{:S(2)}) copy-start(bf16[2048,1024]{1,0:T(8,128)(2,1)} %param.9) | copy-start | bytes 12582916
Sparse Core Ops, SparseCore 0:
  11.3 25.0 all-gather.5
  39.0 46.7 all-gather.3
